TPU v7x, 256 devices: a whole 4x4x8 slice. The times are simulated.
256 devices in a mesh: pipe: 2 (over x_hi), dp: 128 (over x_lo, z, y, core).
Axes of the slice: x: 4 (x_hi: 2, x_lo: 2; x = x_hi * 2 + x_lo), y: 4, z: 8, core: 2. Of those that a mesh axis runs over, the one named last changes fastest.
Arguments:
- images: bfloat16 [256, 1024, 384], P('dp'), may hold values from -6 to 6
- dw_kernel: bfloat16 [2, 49, 384], P('pipe'), may hold values from -0.875 to 0.875
- dw_bias: bfloat16 [2, 384], P('pipe'), may hold values from -3 to 3
- norm_gain: bfloat16 [2, 384], P('pipe'), may hold values from 0.5 to 1.5
- norm_bias: bfloat16 [2, 384], P('pipe'), may hold values from -3 to 3
- w_in: bfloat16 [2, 384, 1536], P('pipe'), may hold values from -0.3125 to 0.3125
- b_in: bfloat16 [2, 1536], P('pipe'), may hold values from -3 to 3
- w_out: bfloat16 [2, 1536, 384], P('pipe'), may hold values from -0.15625 to 0.15625
- b_out: bfloat16 [2, 384], P('pipe'), may hold values from -3 to 3
- layer_scale: bfloat16 [2, 384], P('pipe'), may hold values from 0.29882812 to 1
- image_embed: bfloat16 [1024, 1024], P(('pipe', 'dp')), may hold values from -8 to 8
- text_embed: bfloat16 [1024, 1024], P('dp'), may hold values from -8 to 8
Outputs:
- section_out: bfloat16 [2, 256, 1024, 384], P('pipe', 'dp')
- row_lse: float32 [1024], P(('pipe', 'dp'))
- col_lse: float32 [1024], P('dp')
- grad_image: float32 [1024, 1024], P(('pipe', 'dp'))
- grad_text: float32 [1024, 1024], P('dp')
All inputs are finite; a program needn't handle non-finite values.
Results may differ from a plain program's by a relative error of at most 0.0055.
Values may be sent and summed in bfloat16 or wider, within the bound.
A program may use at most 128 MiB of HBM per device.

v0:
```python
import math

import jax
import jax.numpy as jnp
from jax import lax
from jax.sharding import PartitionSpec as P


def passed_along(block, axis, distance):
    devices = range(lax.axis_size(axis))
    route = [(i - distance, i) for i in devices if i - distance in devices]
    return lax.ppermute(block, axis, route)


def combined_all(part, axis, combine):
    gathered = jax.tree.map(lambda a: lax.all_gather(a, axis), part)

    def take(source):
        return jax.tree.map(lambda a: lax.dynamic_index_in_dim(a, source, 0, False), gathered)

    return lax.fori_loop(
        1, lax.axis_size(axis), lambda source, state: combine(state, take(source)), take(0)
    )


def convnext_block(feature, params):
    dw_kernel, dw_bias, norm_gain, norm_bias, w_in, b_in, w_out, b_out, layer_scale = params
    count, positions, channels = feature.shape
    side = math.isqrt(positions)
    width = math.isqrt(dw_kernel.shape[0])
    grid = feature.reshape(count, side, side, channels)
    kernel = dw_kernel.reshape(width, width, 1, channels)
    conv = lax.conv_general_dilated(
        grid,
        kernel,
        (1, 1),
        ((width // 2, width // 2), (width // 2, width // 2)),
        dimension_numbers=("NHWC", "HWIO", "NHWC"),
        feature_group_count=channels,
        preferred_element_type=jnp.float32,
    )
    conv = conv.reshape(count * positions, channels) + dw_bias.astype(jnp.float32)
    center = conv - jnp.mean(conv, axis=1, keepdims=True)
    spread = jnp.mean(center * center, axis=1, keepdims=True)
    normed = (
        center * lax.rsqrt(spread + 1e-06) * norm_gain.astype(jnp.float32)
        + norm_bias.astype(jnp.float32)
    ).astype(jnp.bfloat16)
    hidden = jnp.dot(normed, w_in, preferred_element_type=jnp.float32) + b_in.astype(jnp.float32)
    hidden = jax.nn.gelu(hidden, approximate=False).astype(jnp.bfloat16)
    branch = jnp.dot(hidden, w_out, preferred_element_type=jnp.float32) + b_out.astype(jnp.float32)
    result = (
        feature.reshape(count * positions, channels).astype(jnp.float32)
        + layer_scale.astype(jnp.float32) * branch
    )
    return result.astype(jnp.bfloat16).reshape(count, positions, channels)


def unit_rows(values):
    wide = values.astype(jnp.float32)
    return (wide * lax.rsqrt(jnp.sum(wide * wide, axis=1, keepdims=True) + 1e-06)).astype(
        jnp.bfloat16
    )


def merge_stats(first, second):
    top = jnp.maximum(first[0], second[0])
    return (top, first[1] * jnp.exp(first[0] - top) + second[1] * jnp.exp(second[0] - top))


def local(
    images,
    dw_kernel,
    dw_bias,
    norm_gain,
    norm_bias,
    w_in,
    b_in,
    w_out,
    b_out,
    layer_scale,
    image_embed,
    text_embed,
):
    section = lax.axis_index("pipe")
    sections = lax.axis_size("pipe")
    micro = images.shape[0]
    params = (dw_kernel, dw_bias, norm_gain, norm_bias, w_in, b_in, w_out, b_out, layer_scale)
    own = tuple((p[0] for p in params))

    def tick(step, carry):
        incoming, record = carry
        fresh = lax.dynamic_slice_in_dim(images, jnp.clip(step, 0, micro - 1), 1, 0)
        source = jnp.where(section == 0, fresh, incoming)
        result = convnext_block(source, own)
        slot = step - section
        valid = jnp.logical_and(slot >= 0, slot < micro)
        place = jnp.clip(slot, 0, micro - 1)
        before = lax.dynamic_slice_in_dim(record, place, 1, 0)
        record = lax.dynamic_update_slice_in_dim(record, jnp.where(valid, result, before), place, 0)
        incoming = passed_along(result, "pipe", 1)
        return (incoming, record)

    start_state = (
        jnp.zeros((1,) + images.shape[1:], jnp.bfloat16),
        jnp.zeros(images.shape, jnp.bfloat16),
    )
    finished = lax.fori_loop(0, micro + sections - 1, tick, start_state)
    section_out = finished[1][None]
    image_unit = unit_rows(image_embed)
    text_unit = unit_rows(text_embed)
    rows = image_unit.shape[0]
    shard = text_unit.shape[0]
    groups = lax.axis_size("dp")
    pairs = groups * shard
    all_text = lax.all_gather(text_unit, "dp", axis=0, tiled=True)
    logits = 100.0 * jnp.einsum(
        "re,te->rt", image_unit, all_text, preferred_element_type=jnp.float32
    )
    row_top = jnp.max(logits, axis=1)
    row_lse = row_top + jnp.log(jnp.sum(jnp.exp(logits - row_top[:, None]), axis=1))
    first_row = (section * groups + lax.axis_index("dp")) * rows
    first_text = lax.axis_index("dp") * shard
    col_top = jnp.max(logits, axis=0)
    col_total = jnp.sum(jnp.exp(logits - col_top[None, :]), axis=0)
    merged_top, merged_total = combined_all((col_top, col_total), ("pipe", "dp"), merge_stats)
    col_lse = merged_top + jnp.log(merged_total)
    col_out = lax.dynamic_slice_in_dim(col_lse, first_text, shard, 0)
    row_ids = first_row + lax.iota(jnp.int32, rows)
    col_ids = lax.iota(jnp.int32, pairs)
    paired = (row_ids[:, None] == col_ids[None, :]).astype(jnp.float32)
    dlogits = (
        jnp.exp(logits - row_lse[:, None]) + jnp.exp(logits - col_lse[None, :]) - 2.0 * paired
    ).astype(jnp.bfloat16)
    grad_image = 100.0 * jnp.dot(dlogits, all_text, preferred_element_type=jnp.float32)
    partial_rows = lax.psum_scatter(
        100.0 * jnp.einsum("rt,re->te", dlogits, image_unit, preferred_element_type=jnp.float32),
        "dp",
        scatter_dimension=0,
        tiled=True,
    )
    grad_text = lax.psum(partial_rows, "pipe")
    return (section_out, row_lse, col_out, grad_image, grad_text)


def solution(mesh):
    in_specs = (
        P("dp", None, None),
        P("pipe", None, None),
        P("pipe", None),
        P("pipe", None),
        P("pipe", None),
        P("pipe", None, None),
        P("pipe", None),
        P("pipe", None, None),
        P("pipe", None),
        P("pipe", None),
        P(("pipe", "dp"), None),
        P("dp", None),
    )
    out_specs = (
        P("pipe", "dp", None, None),
        P(("pipe", "dp")),
        P("dp"),
        P(("pipe", "dp"), None),
        P("dp", None),
    )
    return jax.shard_map(local, mesh=mesh, in_specs=in_specs, out_specs=out_specs, check_vma=False)
```

profile of v0, /device:TPU:6, one launch (start us, length us, event | category | flops | bytes accessed | tf_op | source)
XLA Modules:
  0.0 1268.7 jit_solution(10016299459213593791)
XLA Ops:
  8.1 1.4 fusion.51
  10.4 216.0 %all-gather.6.cloned.1.call-done = bf16[1024,1024]{1,0:T(8,128)(2,1)} async-done(((bf16[8,1024]{1,0:T(8,128)(2,1)}), bf16[1024,1024]{1,0:T(8,128)(2,1)}) %all-gather.6.cloned.1.call-update) | async-done | bytes 2097168 | tf_op jit(solution)/shard_map/all_gather | solution.py:116
  226.4 2.9 fusion.56
  229.3 1.4 exponential_reduce_fusion
  230.8 100.2 %all-gather.8.cloned.1.call-done = f32[262144]{0:T(1024)} async-done(((f32[1024]{0:T(1024)}), f32[262144]{0:T(1024)}) %all-gather.8.cloned.1.call-update) | async-done | bytes 1048592 | tf_op jit(solution)/shard_map/all_gather | solution.py:16
  331.0 1.5 reshape.163
  332.5 103.8 %all-gather.10.cloned.1.call-done = f32[262144]{0:T(1024)} async-done(((f32[1024]{0:T(1024)}), f32[262144]{0:T(1024)}) %all-gather.10.cloned.1.call-update) | async-done | bytes 1048592 | tf_op jit(solution)/shard_map/all_gather | solution.py:16
  437.0 1.4 reshape.164
  438.4 15.0 %while.34 = (s32[]{:T(128)}, f32[1024]{0:T(1024)S(1)}, f32[1024]{0:T(1024)S(1)}, f32[256,1024]{1,0:T(8,128)S(1)}, f32[256,1024]{1,0:T(8,128)S(1)}, /*index=5*/s32[]{:T(128)}, s32[]{:T(128)}, s32[]{:T(128)}) while((s32[]{:T(128)}, f32[1024]{0:T(1024)S(1)}, f32[1024]{0:T(1024)S(1)}, f32[256,1024]{1,0:T(8,128)S(1)}, ...), condition=%wide.region_11.12_spmd, body=%wide.region_10.11_spmd.sunk | while | flops 6149 | bytes 41083 | solution.py:21
  453.5 2.8 convolution_multiply_fusion
  458.1 567.2 %reduce-scatter.2.cloned.1.call-done = f32[8,1024]{1,0:T(8,128)} async-done(((f32[1024,1024]{1,0:T(8,128)}), f32[8,1024]{1,0:T(8,128)}) %reduce-scatter.2.cloned.1.call-update) | async-done | bytes 32784 | tf_op jit(solution)/shard_map/reduce_scatter | solution.py:136
  1025.3 9.6 psum.7
  1035.0 1.3 broadcast_in_dim.42
  1036.3 225.8 %while.33 = (s32[]{:T(128)}, bf16[1,1024,384]{2,1,0:T(8,128)(2,1)S(1)}, bf16[2,1024,384]{2,1,0:T(8,128)(2,1)}, pred[]{:T(512)}, bf16[2,1024,384]{2,1,0:T(8,128)(...) while((s32[]{:T(128)}, ...), condition=%wide.region_3.4_spmd, body=%wide.region_0.3_spmd.sunk | while | flops 2561720832 | bytes 24583492 | solution.py:108
  1036.4 1.2 dynamic-slice_select_fusion.2
  1037.6 24.1 %add_reduce_fusion.2 = (f32[32,32]{1,0:T(8,128)S(1)}, f32[1,32,32,384]{3,0,2,1:T(1,128)S(1)}) fusion(f32[384]{0:T(512)S(1)} %convert_element_type.178, bf16[7,7,1,384]{3,2,1,0:T(2,128)(2,1)S(1)} %reshape_squeeze.10, bf16[1,32,32,384]{3,2,1,0:T(8,128)(2,1)S(1)} %bitcast.45), kind=kOutput, calls=%fused_computation.32.clone.1 | convolution fusion | flops 35302400 | bytes 2402560 | tf_op jit(solution)/shard_map/while/body/eval_jaxpr/conv_general_dilated | solution.py:33
  1061.8 15.3 %multiply_reduce_fusion.2 = f32[32,32]{1,0:T(8,128)S(1)} fusion(f32[1,32,32,384]{3,0,2,1:T(1,128)S(1)} %get-tuple-element.609, f32[32,32]{1,0:T(8,128)S(1)} %broadcast_multiply_fusion.2, f32[384]{0:T(512)S(1)} %convert_element_type.178), kind=kLoop, calls=%fused_computation.29.clone.1 | loop fusion | flops 1571840 | bytes 1582592 | tf_op jit(solution)/shard_map/while/body/eval_jaxpr/reduce_sum | solution.py:44
  1077.8 18.4 %select_dynamic-update-slice_fusion.2 = (bf16[2,1024,384]{2,1,0:T(8,128)(2,1)}, bf16[1,1024,384]{2,1,0:T(8,128)(2,1)S(1)}) fusion(bf16[2,1024,384]{2,1,0:T(8,128)(2,1)} %get-tuple-element.642, s32[]{:T(128)S(6)} %min.20, pred[]{:T(512)S(6)} %and.11, f32[384]{0:T(512)S(1)} %convert_element_type.177, bf16[1536,384]{1,0:T(8,128)(2,1)} %get-tuple-element.670, ...), kind=kOutput, calls=%fused_computation.33.clone.1 | convolution fusion | flops 2522087424 | bytes 6300677 | tf_op jit(solution)/shard_map/while/body/eval_jaxpr/dot_general | solution.py:51
  1096.2 1.3 collective-permute-start
  1097.5 14.1 %collective-permute-done = bf16[1,1024,384]{2,1,0:T(8,128)(2,1)S(1)} collective-permute-done((bf16[1,1024,384]{2,1,0:T(8,128)(2,1)S(1)}, bf16[1,1024,384]{2,1,0:T(8,128)(2,1)S(1)}, u32[]{:S(2)}, u32[]{:S(2)}) %collective-permute-start) | collective-permute-done | bytes 786464 | tf_op jit(solution)/shard_map/while/body/eval_jaxpr/ppermute | solution.py:12
  1111.7 1.2 dynamic-slice_select_fusion.2
  1112.9 24.1 %add_reduce_fusion.2 = (f32[32,32]{1,0:T(8,128)S(1)}, f32[1,32,32,384]{3,0,2,1:T(1,128)S(1)}) fusion(f32[384]{0:T(512)S(1)} %convert_element_type.178, bf16[7,7,1,384]{3,2,1,0:T(2,128)(2,1)S(1)} %reshape_squeeze.10, bf16[1,32,32,384]{3,2,1,0:T(8,128)(2,1)S(1)} %bitcast.45), kind=kOutput, calls=%fused_computation.32.clone.1 | convolution fusion | flops 35302400 | bytes 2402560 | tf_op jit(solution)/shard_map/while/body/eval_jaxpr/conv_general_dilated | solution.py:33
  1137.1 15.3 %multiply_reduce_fusion.2 = f32[32,32]{1,0:T(8,128)S(1)} fusion(f32[1,32,32,384]{3,0,2,1:T(1,128)S(1)} %get-tuple-element.609, f32[32,32]{1,0:T(8,128)S(1)} %broadcast_multiply_fusion.2, f32[384]{0:T(512)S(1)} %convert_element_type.178), kind=kLoop, calls=%fused_computation.29.clone.1 | loop fusion | flops 1571840 | bytes 1582592 | tf_op jit(solution)/shard_map/while/body/eval_jaxpr/reduce_sum | solution.py:44
  1153.1 18.4 %select_dynamic-update-slice_fusion.2 = (bf16[2,1024,384]{2,1,0:T(8,128)(2,1)}, bf16[1,1024,384]{2,1,0:T(8,128)(2,1)S(1)}) fusion(bf16[2,1024,384]{2,1,0:T(8,128)(2,1)} %get-tuple-element.642, s32[]{:T(128)S(6)} %min.20, pred[]{:T(512)S(6)} %and.11, f32[384]{0:T(512)S(1)} %convert_element_type.177, bf16[1536,384]{1,0:T(8,128)(2,1)} %get-tuple-element.670, ...), kind=kOutput, calls=%fused_computation.33.clone.1 | convolution fusion | flops 2522087424 | bytes 6300677 | tf_op jit(solution)/shard_map/while/body/eval_jaxpr/dot_general | solution.py:51
  1171.5 1.3 collective-permute-start
  1172.8 14.1 %collective-permute-done = bf16[1,1024,384]{2,1,0:T(8,128)(2,1)S(1)} collective-permute-done((bf16[1,1024,384]{2,1,0:T(8,128)(2,1)S(1)}, bf16[1,1024,384]{2,1,0:T(8,128)(2,1)S(1)}, u32[]{:S(2)}, u32[]{:S(2)}) %collective-permute-start) | collective-permute-done | bytes 786464 | tf_op jit(solution)/shard_map/while/body/eval_jaxpr/ppermute | solution.py:12
  1186.9 1.2 dynamic-slice_select_fusion.2
  1188.2 24.1 %add_reduce_fusion.2 = (f32[32,32]{1,0:T(8,128)S(1)}, f32[1,32,32,384]{3,0,2,1:T(1,128)S(1)}) fusion(f32[384]{0:T(512)S(1)} %convert_element_type.178, bf16[7,7,1,384]{3,2,1,0:T(2,128)(2,1)S(1)} %reshape_squeeze.10, bf16[1,32,32,384]{3,2,1,0:T(8,128)(2,1)S(1)} %bitcast.45), kind=kOutput, calls=%fused_computation.32.clone.1 | convolution fusion | flops 35302400 | bytes 2402560 | tf_op jit(solution)/shard_map/while/body/eval_jaxpr/conv_general_dilated | solution.py:33
  1212.4 15.3 %multiply_reduce_fusion.2 = f32[32,32]{1,0:T(8,128)S(1)} fusion(f32[1,32,32,384]{3,0,2,1:T(1,128)S(1)} %get-tuple-element.609, f32[32,32]{1,0:T(8,128)S(1)} %broadcast_multiply_fusion.2, f32[384]{0:T(512)S(1)} %convert_element_type.178), kind=kLoop, calls=%fused_computation.29.clone.1 | loop fusion | flops 1571840 | bytes 1582592 | tf_op jit(solution)/shard_map/while/body/eval_jaxpr/reduce_sum | solution.py:44
  1228.3 18.4 %select_dynamic-update-slice_fusion.2 = (bf16[2,1024,384]{2,1,0:T(8,128)(2,1)}, bf16[1,1024,384]{2,1,0:T(8,128)(2,1)S(1)}) fusion(bf16[2,1024,384]{2,1,0:T(8,128)(2,1)} %get-tuple-element.642, s32[]{:T(128)S(6)} %min.20, pred[]{:T(512)S(6)} %and.11, f32[384]{0:T(512)S(1)} %convert_element_type.177, bf16[1536,384]{1,0:T(8,128)(2,1)} %get-tuple-element.670, ...), kind=kOutput, calls=%fused_computation.33.clone.1 | convolution fusion | flops 2522087424 | bytes 6300677 | tf_op jit(solution)/shard_map/while/body/eval_jaxpr/dot_general | solution.py:51
  1246.7 1.3 collective-permute-start
  1248.0 14.1 %collective-permute-done = bf16[1,1024,384]{2,1,0:T(8,128)(2,1)S(1)} collective-permute-done((bf16[1,1024,384]{2,1,0:T(8,128)(2,1)S(1)}, bf16[1,1024,384]{2,1,0:T(8,128)(2,1)S(1)}, u32[]{:S(2)}, u32[]{:S(2)}) %collective-permute-start) | collective-permute-done | bytes 786464 | tf_op jit(solution)/shard_map/while/body/eval_jaxpr/ppermute | solution.py:12
  (602 shorter events, 13.4 us)
Async XLA Ops:
  7.2 446.3 %copy-start.3 = (bf16[4,1024]{1,0:T(4,128)(2,1)S(1)}, bf16[4,1024]{1,0:T(4,128)(2,1)}, u32[]{:S(2)}) copy-start(bf16[4,1024]{1,0:T(4,128)(2,1)} %param.26) | copy-start | bytes 24580
  7.2 219.2 %all-gather.6.cloned.1.call-start = ((), (), s32[]{:S(2)}) async-start(), calls=%async_computation.1 | async-start | bytes 2113536 | tf_op jit(solution)/shard_map/all_gather | solution.py:116
  9.5 321.5 %all-gather.8.cloned.1.call-start = ((), (), s32[]{:S(2)}) async-start(), calls=%async_computation.3 | async-start | bytes 1052672 | tf_op jit(solution)/shard_map/all_gather | solution.py:16
  229.3 207.0 %all-gather.10.cloned.1.call-start = ((), (), s32[]{:S(2)}) async-start(), calls=%async_computation.4 | async-start | bytes 1052672 | tf_op jit(solution)/shard_map/all_gather | solution.py:16
  230.7 794.6 %reduce-scatter.2.cloned.1.call-start = ((), (), s32[]{:S(2)}) async-start(), calls=%async_computation.2 | async-start | bytes 4227072 | tf_op jit(solution)/shard_map/reduce_scatter | solution.py:136
  230.8 226.3 %copy-start.5 = (f32[4]{0:T(128)}, f32[4]{0:T(128)S(1)}, u32[]{:S(2)}) copy-start(f32[4]{0:T(128)S(1)} %log_add_fusion.1) | copy-start | bytes 52
  331.0 107.3 %slice-start = ((f32[262144]{0:T(1024)}), f32[1024]{0:T(1024)S(1)}, s32[]{:S(2)}) async-start(f32[262144]{0:T(1024)} %all-gather.8.cloned.1.call-done), calls=%async_computation.5 | async-start | bytes 8192 | tf_op jit(solution)/shard_map/jit(dynamic_index_in_dim)/dynamic_slice | solution.py:19
  453.4 2.9 copy-start.6
  453.4 2.9 copy-start.7
  453.5 2.9 copy-start.8
  453.5 2.9 copy-start.9
  453.5 2.9 copy-start.10
  453.5 3.0 copy-start.4
  453.5 3.6 copy-start.1
  456.3 580.0 %copy-start.2 = (bf16[1,49,384]{2,1,0:T(8,128)(2,1)S(1)}, bf16[1,49,384]{2,1,0:T(8,128)(2,1)}, u32[]{:S(2)}) copy-start(bf16[1,49,384]{2,1,0:T(8,128)(2,1)} %param.17) | copy-start | bytes 112900
  1037.6 24.1 %copy-start = (bf16[1,1024,384]{2,1,0:T(8,128)(2,1)}, bf16[1,1024,384]{2,1,0:T(8,128)(2,1)S(1)}, u32[]{:S(2)}) copy-start(bf16[1,1024,384]{2,1,0:T(8,128)(2,1)S(1)} %dynamic-slice_select_fusion.2) | copy-start | bytes 2359300 | tf_op jit(solution)/shard_map/while
  1096.2 15.4 %collective-permute-start = (bf16[1,1024,384]{2,1,0:T(8,128)(2,1)S(1)}, bf16[1,1024,384]{2,1,0:T(8,128)(2,1)S(1)}, u32[]{:S(2)}, u32[]{:S(2)}) collective-permute-start(bf16[1,1024,384]{2,1,0:T(8,128)(2,1)S(1)} %get-tuple-element.611), channel_id=1, source_target_pairs={{0,128},{1,129},{2,130},{3,131},{4,132},{5,133},{6,134},{7,135},{8... | collective-permute-start | bytes 2359304 | tf_op jit(solution)/shard_map/while/body/eval_jaxpr/ppermute | solution.py:12
  1112.9 24.1 %copy-start = (bf16[1,1024,384]{2,1,0:T(8,128)(2,1)}, bf16[1,1024,384]{2,1,0:T(8,128)(2,1)S(1)}, u32[]{:S(2)}) copy-start(bf16[1,1024,384]{2,1,0:T(8,128)(2,1)S(1)} %dynamic-slice_select_fusion.2) | copy-start | bytes 2359300 | tf_op jit(solution)/shard_map/while
  1171.5 15.4 %collective-permute-start = (bf16[1,1024,384]{2,1,0:T(8,128)(2,1)S(1)}, bf16[1,1024,384]{2,1,0:T(8,128)(2,1)S(1)}, u32[]{:S(2)}, u32[]{:S(2)}) collective-permute-start(bf16[1,1024,384]{2,1,0:T(8,128)(2,1)S(1)} %get-tuple-element.611), channel_id=1, source_target_pairs={{0,128},{1,129},{2,130},{3,131},{4,132},{5,133},{6,134},{7,135},{8... | collective-permute-start | bytes 2359304 | tf_op jit(solution)/shard_map/while/body/eval_jaxpr/ppermute | solution.py:12
  1188.2 24.1 %copy-start = (bf16[1,1024,384]{2,1,0:T(8,128)(2,1)}, bf16[1,1024,384]{2,1,0:T(8,128)(2,1)S(1)}, u32[]{:S(2)}) copy-start(bf16[1,1024,384]{2,1,0:T(8,128)(2,1)S(1)} %dynamic-slice_select_fusion.2) | copy-start | bytes 2359300 | tf_op jit(solution)/shard_map/while
  1246.7 15.4 %collective-permute-start = (bf16[1,1024,384]{2,1,0:T(8,128)(2,1)S(1)}, bf16[1,1024,384]{2,1,0:T(8,128)(2,1)S(1)}, u32[]{:S(2)}, u32[]{:S(2)}) collective-permute-start(bf16[1,1024,384]{2,1,0:T(8,128)(2,1)S(1)} %get-tuple-element.611), channel_id=1, source_target_pairs={{0,128},{1,129},{2,130},{3,131},{4,132},{5,133},{6,134},{7,135},{8... | collective-permute-start | bytes 2359304 | tf_op jit(solution)/shard_map/while/body/eval_jaxpr/ppermute | solution.py:12
Sparse Core Ops, SparseCore 0:
  10.5 215.8 all-gather.5
  230.7 100.3 all-gather.7
  335.3 100.9 all-gather.9
  456.4 568.8 reduce-scatter.1
where the time goes:
time: 1280 us; the launch traced here: 1270 us
  waiting for transfers between devices  1030 us (80%)
  matrix products  134 us (10%)
  other arithmetic  58.5 us (5%)
  between operations  13.9 us (1%)
    reduce_scatter x1, waiting for transfers between devices, local(): lax.psum_scatter(100.0 * jnp.einsum('rt,re->te', dlogits, image_unit, pre...  567 us
    all_gather x1, waiting for transfers between devices, local(): all_text = lax.all_gather(text_unit, 'dp', axis=0, tiled=True)  216 us
    all_gather x2, waiting for transfers between devices, combined_all(): gathered = jax.tree.map(lambda a: lax.all_gather(a, axis), part)  204 us
    conv_general_dilated x3, matrix products, convnext_block(): lax.conv_general_dilated(grid, kernel, (1, 1), ((width // 2, width // 2),...  72.2 us
    dot_general x3, matrix products, convnext_block(): jnp.dot(hidden, w_out, preferred_element_type=jnp.float32)  55.2 us
    reduce_sum x3, other arithmetic, convnext_block(): spread = jnp.mean(center * center, axis=1, keepdims=True)  46 us
    ppermute x3, waiting for transfers between devices, passed_along(): return lax.ppermute(block, axis, route)  42.3 us
  transfers between devices with their start and end apart: 7, of which 7 were waited for; matrix products, arithmetic and copies ran while one was open for 0% of the time, Pallas kernels for 0%

commit v1 on v0

v1 whole, which is shorter than its diff:
```python
import functools

import jax
import jax.numpy as jnp
from jax import lax
from jax.experimental import pallas as pl
from jax.experimental.pallas import tpu as pltpu
from jax.sharding import PartitionSpec as P

MESH = pl.DeviceIdType.MESH
F32 = jnp.float32
BF16 = jnp.bfloat16

N_Z, N_Y = 8, 4
GROUP = 16
SIDE = 32
LANES = 128
STRIP = 8
STRIPS = SIDE // STRIP
POS = STRIP * SIDE
LEFT = 8
CHUNK = 256


def kernel(
    images, dw_kernel, dw_bias, norm_gain, norm_bias, w_in, b_in, w_out, b_out, layer_scale,
    image_embed, text_embed,
    out, row_out, col_out, grad_image, grad_text,
    src, outbuf, xpad, taps, conv, normed, branch, w_in_v, w_out_v,
    imgbuf, txtbuf, imgf, img2, txt2, logit, logit_t, rowst, colst,
    gi_send, gi_recv, gt_send, gt_recv, gt_half, gt_other,
    load_sem, store_sem, strip_send, strip_recv, img_send, img_recv, txt_send, txt_recv,
    row_send, row_recv, col_send, col_recv, gis_sem, gir_sem, gts_sem, gtr_sem, half_send, half_recv,
):
    sec = lax.axis_index("pipe")
    dp = lax.axis_index("dp")
    core = lax.rem(dp, 2)
    y = lax.rem(lax.div(dp, 2), N_Y)
    z = lax.rem(lax.div(dp, 2 * N_Y), N_Z)
    x_lo = lax.div(dp, 2 * N_Y * N_Z)
    me_row = x_lo * 8 + y * 2 + core
    me_col = sec * N_Z + z
    micro = src.shape[0]
    channels = src.shape[2]
    tiles = channels // LANES
    hidden = w_in_v.shape[1]
    total = micro * STRIPS

    def row_peer(j):
        return (sec, ((lax.div(j, 8) * N_Z + z) * N_Y + lax.rem(lax.div(j, 2), N_Y)) * 2 + lax.rem(j, 2))

    def col_peer(j):
        return (lax.div(j, N_Z), ((x_lo * N_Z + lax.rem(j, N_Z)) * N_Y + y) * 2 + core)

    def text_peer(j):
        return (sec, ((x_lo * N_Z + j) * N_Y + y) * 2 + core)

    partner = (1 - sec, dp)

    def remote(source, target, send, recv, device):
        return pltpu.make_async_remote_copy(
            src_ref=source, dst_ref=target, send_sem=send, recv_sem=recv,
            device_id=device, device_id_type=MESH,
        )

    def others(count, me, act):
        def one(j, carry):
            @pl.when(j != me)
            def _():
                act(j)
            return carry
        lax.fori_loop(0, count, one, 0)

    load_x = pltpu.make_async_copy(images, src, load_sem.at[0])
    load_a = pltpu.make_async_copy(w_in.at[0], w_in_v, load_sem.at[1])
    load_b = pltpu.make_async_copy(w_out.at[0], w_out_v, load_sem.at[2])

    @pl.when(sec == 0)
    def _():
        load_x.start()
    load_a.start()
    load_b.start()

    barrier = pltpu.get_barrier_semaphore()
    others(GROUP, me_row, lambda j: pl.semaphore_signal(
        barrier, inc=1, device_id=row_peer(j), device_id_type=MESH))
    others(GROUP, me_col, lambda j: pl.semaphore_signal(
        barrier, inc=1, device_id=col_peer(j), device_id_type=MESH))

    def unit(values):
        wide = values.astype(F32)
        return (wide * lax.rsqrt(jnp.sum(wide * wide, axis=1, keepdims=True) + 1e-06)).astype(BF16)

    imgbuf[me_row] = unit(image_embed[...])
    txtbuf[z] = unit(text_embed[...])

    xpad[:, :, 0:3] = jnp.zeros(xpad.shape[:2] + (3,) + xpad.shape[3:], F32)
    xpad[:, :, SIDE + 3:SIDE + 6] = jnp.zeros(xpad.shape[:2] + (3,) + xpad.shape[3:], F32)
    xpad[:, :, :, 0:LEFT] = jnp.zeros(xpad.shape[:3] + (LEFT, LANES), F32)
    xpad[:, :, :, LEFT + SIDE:] = jnp.zeros(xpad.shape[:3] + (8, LANES), F32)
    kv = dw_kernel[0].astype(F32)
    for c in range(tiles):
        for t in range(49):
            taps[c, t] = jnp.broadcast_to(kv[t:t + 1, c * LANES:(c + 1) * LANES], (8, LANES))

    pl.semaphore_wait(barrier, 2 * (GROUP - 1))

    def img_copy(slot, j):
        return remote(imgbuf.at[slot], imgbuf.at[slot], img_send.at[j], img_recv.at[slot], row_peer(j))

    def txt_copy(slot, j):
        return remote(txtbuf.at[slot], txtbuf.at[slot], txt_send.at[j], txt_recv.at[slot], text_peer(j))

    def row_copy(slot, j):
        return remote(rowst.at[slot], rowst.at[slot], row_send.at[j], row_recv.at[slot], row_peer(j))

    def col_copy(slot, j):
        return remote(colst.at[slot], colst.at[slot], col_send.at[j], col_recv.at[slot], col_peer(j))

    def gi_copy(slot, j):
        return remote(gi_send.at[j], gi_recv.at[slot], gis_sem.at[j], gir_sem.at[slot], row_peer(j))

    def gt_copy(slot, j):
        return remote(gt_send.at[j], gt_recv.at[slot], gts_sem.at[j], gtr_sem.at[slot], text_peer(j))

    half_copy = remote(gt_half, gt_other, half_send, half_recv, partner)

    others(GROUP, me_row, lambda j: img_copy(me_row, j).start())
    others(N_Z, z, lambda j: txt_copy(z, j).start())

    def finish(copy):
        copy.wait_send()
        copy.wait_recv()

    lane = lax.broadcasted_iota(jnp.int32, (1, LANES), 1)
    low = lane < 64

    def loss_logits():
        others(GROUP, me_row, lambda j: finish(img_copy(j, j)))
        others(N_Z, z, lambda j: finish(txt_copy(j, j)))
        for j in range(GROUP):
            imgf[4 * j:4 * j + 4] = imgbuf[j].astype(F32)
        img = imgf[...].astype(BF16)
        img2[0:64] = img
        img2[64:128] = img
        for j in range(N_Z):
            imgf[8 * j:8 * j + 8] = txtbuf[j].astype(F32)
        txt = imgf[...].astype(BF16)
        txt2[0:64] = txt
        txt2[64:128] = txt
        dims = (((1,), (1,)), ((), ()))
        a = 100.0 * lax.dot_general(img2[0:64], txt2[...], dims, preferred_element_type=F32)
        b = 100.0 * lax.dot_general(txt2[0:64], img2[...], dims, preferred_element_type=F32)
        logit[...] = a
        logit_t[...] = b

        def stats(values):
            top = jnp.max(values, axis=0, keepdims=True)
            return jnp.where(low, top, jnp.sum(jnp.exp(values - top), axis=0, keepdims=True))

        colst[me_col] = stats(a)
        rowst[me_row] = stats(b)
        others(GROUP, me_row, lambda j: row_copy(me_row, j).start())
        others(GROUP, me_col, lambda j: col_copy(me_col, j).start())

    def merged(ref):
        parts = [ref[j] for j in range(GROUP)]
        top = functools.reduce(jnp.maximum, parts)
        add = functools.reduce(
            jnp.add, [pltpu.roll(p, 64, 1) * jnp.exp(jnp.where(low, p - top, 0.0)) for p in parts])
        lse = top + jnp.log(jnp.where(low, add, 1.0))
        return jnp.where(low, lse, pltpu.roll(lse, 64, 1))

    def upright(row):
        here = lax.broadcasted_iota(jnp.int32, (64, LANES), 0) == lax.broadcasted_iota(jnp.int32, (64, LANES), 1)
        return jnp.sum(jnp.where(here, row, 0.0), axis=1, keepdims=True)

    def image_ids(r):
        j = r >> 2
        peer = (((j >> 3) * N_Z + z) * N_Y + ((j >> 1) & 3)) * 2 + (j & 1)
        return (sec * 128 + peer) * 4 + (r & 3)

    def text_ids(r):
        return (((x_lo * N_Z + (r >> 3)) * N_Y + y) * 2 + core) * 8 + (r & 7)

    def loss_grads():
        others(GROUP, me_row, lambda j: finish(row_copy(j, j)))
        others(GROUP, me_col, lambda j: finish(col_copy(j, j)))
        row_lse = merged(rowst)
        col_lse = merged(colst)
        row_out[...] = pltpu.roll(row_lse, LANES - 4 * me_row, 1)[:, 0:4]
        col_out[...] = pltpu.roll(col_lse, LANES - 8 * z, 1)[:, 0:8]
        up = lax.broadcasted_iota(jnp.int32, (64, LANES), 0)
        across = lax.broadcasted_iota(jnp.int32, (64, LANES), 1)
        inside = across < 64
        a = logit[...]
        pair = image_ids(up) == text_ids(across)
        d = jnp.exp(a - upright(row_lse)) + jnp.exp(a - col_lse) - jnp.where(pair, 2.0, 0.0)
        d = jnp.where(inside, d, 0.0).astype(BF16)
        b = logit_t[...]
        pair_t = text_ids(up) == image_ids(across)
        dt = jnp.exp(b - row_lse) + jnp.exp(b - upright(col_lse)) - jnp.where(pair_t, 2.0, 0.0)
        dt = jnp.where(inside, dt, 0.0).astype(BF16)
        gi = 100.0 * jnp.dot(d, txt2[...], preferred_element_type=F32)
        gt = 100.0 * jnp.dot(dt, img2[...], preferred_element_type=F32)
        for j in range(GROUP):
            gi_send[j] = gi[4 * j:4 * j + 4]
        for j in range(N_Z):
            gt_send[j] = gt[8 * j:8 * j + 8]
        gi_recv[me_row] = gi_send[me_row]
        gt_recv[z] = gt_send[z]
        others(GROUP, me_row, lambda j: gi_copy(me_row, j).start())
        others(N_Z, z, lambda j: gt_copy(z, j).start())

    def loss_sums():
        others(GROUP, me_row, lambda j: finish(gi_copy(j, j)))
        others(N_Z, z, lambda j: finish(gt_copy(j, j)))
        grad_image[...] = functools.reduce(jnp.add, [gi_recv[j] for j in range(GROUP)])
        gt_half[...] = functools.reduce(jnp.add, [gt_recv[j] for j in range(N_Z)])
        half_copy.start()

    def strip_copy(n):
        i, s = lax.div(n, STRIPS), lax.rem(n, STRIPS)
        rows = pl.ds(pl.multiple_of(s * POS, POS), POS)
        return remote(outbuf.at[i, rows], src.at[i, rows], strip_send.at[n], strip_recv.at[n], (1, dp))

    def store_copy(n):
        i, s = lax.div(n, STRIPS), lax.rem(n, STRIPS)
        rows = pl.ds(pl.multiple_of(s * POS, POS), POS)
        return pltpu.make_async_copy(outbuf.at[i, rows], out.at[0, i, rows], store_sem.at[n])

    def arrive(n):
        i, s = lax.div(n, STRIPS), lax.rem(n, STRIPS)

        @pl.when(sec == 1)
        def _():
            strip_copy(n).wait_recv()
        v = src[i, pl.ds(pl.multiple_of(s * POS, POS), POS)].astype(F32)
        for c in range(tiles):
            xpad[i, c, pl.ds(3 + STRIP * s, STRIP), LEFT:LEFT + SIDE] = (
                v[:, c * LANES:(c + 1) * LANES].reshape(STRIP, SIDE, LANES))

    def block(i, s):
        half = 4

        def convolve(n, carry):
            c, h = lax.div(n, STRIP // half), lax.rem(n, STRIP // half)
            acc = jnp.zeros((half, 4, 8, LANES), F32)
            for dw in range(7):
                start = LEFT - 3 + dw
                xs = xpad[i, c, pl.ds(STRIP * s + half * h, half + 6), start:start + SIDE]
                xs = xs.reshape(half + 6, 4, 8, LANES)
                for dh in range(7):
                    acc = acc + xs[dh:dh + half] * taps[c, dh * 7 + dw]
            rows = pl.ds(pl.multiple_of(h * half * SIDE, half * SIDE), half * SIDE)
            conv[c, rows] = acc.reshape(half * SIDE, LANES)
            return carry

        lax.fori_loop(0, tiles * (STRIP // half), convolve, 0)

        def part(ref, c):
            return ref[0:1, c * LANES:(c + 1) * LANES].astype(F32)

        for q in range(4):
            rows = slice(q * POS // 4, (q + 1) * POS // 4)
            v = [conv[c, rows] + part(dw_bias, c) for c in range(tiles)]
            mean = jnp.sum(functools.reduce(jnp.add, v), axis=1, keepdims=True) * (1.0 / channels)
            v = [a - mean for a in v]
            var = jnp.sum(functools.reduce(jnp.add, [a * a for a in v]), axis=1, keepdims=True) * (1.0 / channels)
            scale = lax.rsqrt(var + 1e-06)
            for c in range(tiles):
                normed[rows, c * LANES:(c + 1) * LANES] = (
                    v[c] * scale * part(norm_gain, c) + part(norm_bias, c)).astype(BF16)

        for n in range(hidden // CHUNK):
            cols = slice(n * CHUNK, (n + 1) * CHUNK)
            h = jnp.dot(normed[...], w_in_v[:, cols], preferred_element_type=F32)
            h = h + b_in[0:1, cols].astype(F32)
            g = (0.5 * h * (1.0 + lax.erf(h * 0.7071067811865476))).astype(BF16)
            p = jnp.dot(g, w_out_v[cols], preferred_element_type=F32)
            if n == 0:
                branch[...] = p
            else:
                branch[...] += p

        for c in range(tiles):
            cols = slice(c * LANES, (c + 1) * LANES)
            x = xpad[i, c, pl.ds(3 + STRIP * s, STRIP), LEFT:LEFT + SIDE].reshape(POS, LANES)
            r = x + part(layer_scale, c) * (branch[:, cols] + part(b_out, c))
            outbuf[i, pl.ds(pl.multiple_of(s * POS, POS), POS), cols] = r.astype(BF16)

    @pl.when(sec == 0)
    def _():
        load_x.wait()
    load_a.wait()
    load_b.wait()

    def step(k, carry):
        i, s = lax.div(k, STRIPS), lax.rem(k, STRIPS)

        @pl.when(k == 2 - 2 * sec)
        def _():
            loss_logits()

        @pl.when(k == 4 - 3 * sec)
        def _():
            loss_grads()

        @pl.when(k == 6 - 3 * sec)
        def _():
            loss_sums()

        @pl.when(s == 0)
        def _():
            arrive(k)

        @pl.when(s < STRIPS - 1)
        def _():
            arrive(k + 1)
        block(i, s)

        @pl.when(sec == 0)
        def _():
            strip_copy(k).start()
        store_copy(k).start()
        return carry

    lax.fori_loop(0, total, step, 0)

    half_copy.wait_send()
    half_copy.wait_recv()
    grad_text[...] = gt_half[...] + gt_other[...]

    def drain(n, carry):
        store_copy(n).wait()

        @pl.when(sec == 0)
        def _():
            strip_copy(n).wait_send()
        return carry

    lax.fori_loop(0, total, drain, 0)


def local(images, dw_kernel, dw_bias, norm_gain, norm_bias, w_in, b_in, w_out, b_out, layer_scale,
          image_embed, text_embed):
    micro, positions, channels = images.shape
    hidden = w_in.shape[2]
    width = image_embed.shape[1]
    rows, shard = image_embed.shape[0], text_embed.shape[0]
    tiles = channels // LANES
    total = micro * STRIPS
    vmem = pl.BlockSpec(memory_space=pltpu.VMEM)
    hbm = pl.BlockSpec(memory_space=pl.ANY)
    dma = pltpu.SemaphoreType.DMA
    section_out, row_lse, col_lse, grad_image, grad_text = pl.pallas_call(
        kernel,
        out_shape=(
            jax.ShapeDtypeStruct((1,) + images.shape, BF16),
            jax.ShapeDtypeStruct((1, rows), F32),
            jax.ShapeDtypeStruct((1, shard), F32),
            jax.ShapeDtypeStruct((rows, width), F32),
            jax.ShapeDtypeStruct((shard, width), F32),
        ),
        in_specs=[hbm, vmem, vmem, vmem, vmem, hbm, vmem, hbm, vmem, vmem, vmem, vmem],
        out_specs=(hbm, vmem, vmem, vmem, vmem),
        scratch_shapes=[
            pltpu.VMEM(images.shape, BF16),
            pltpu.VMEM(images.shape, BF16),
            pltpu.VMEM((micro, tiles, SIDE + 6, LEFT + SIDE + 8, LANES), F32),
            pltpu.VMEM((tiles, 49, 8, LANES), F32),
            pltpu.VMEM((tiles, POS, LANES), F32),
            pltpu.VMEM((POS, channels), BF16),
            pltpu.VMEM((POS, channels), F32),
            pltpu.VMEM((channels, hidden), BF16),
            pltpu.VMEM((hidden, channels), BF16),
            pltpu.VMEM((GROUP, rows, width), BF16),
            pltpu.VMEM((N_Z, shard, width), BF16),
            pltpu.VMEM((64, width), F32),
            pltpu.VMEM((128, width), BF16),
            pltpu.VMEM((128, width), BF16),
            pltpu.VMEM((64, LANES), F32),
            pltpu.VMEM((64, LANES), F32),
            pltpu.VMEM((GROUP, 1, LANES), F32),
            pltpu.VMEM((GROUP, 1, LANES), F32),
            pltpu.VMEM((GROUP, rows, width), F32),
            pltpu.VMEM((GROUP, rows, width), F32),
            pltpu.VMEM((N_Z, shard, width), F32),
            pltpu.VMEM((N_Z, shard, width), F32),
            pltpu.VMEM((shard, width), F32),
            pltpu.VMEM((shard, width), F32),
            dma((3,)), dma((total,)), dma((total,)), dma((total,)),
            dma((GROUP,)), dma((GROUP,)), dma((N_Z,)), dma((N_Z,)),
            dma((GROUP,)), dma((GROUP,)), dma((GROUP,)), dma((GROUP,)),
            dma((GROUP,)), dma((GROUP,)), dma((N_Z,)), dma((N_Z,)),
            dma, dma,
        ],
        compiler_params=pltpu.CompilerParams(
            collective_id=0, has_side_effects=True, vmem_limit_bytes=56 * 1024 * 1024),
        name="sections_and_loss",
    )(images, dw_kernel, dw_bias, norm_gain, norm_bias, w_in, b_in, w_out, b_out, layer_scale,
      image_embed, text_embed)
    return (section_out, row_lse.reshape(rows), col_lse.reshape(shard), grad_image, grad_text)


def solution(mesh):
    in_specs = (
        P("dp", None, None),
        P("pipe", None, None),
        P("pipe", None),
        P("pipe", None),
        P("pipe", None),
        P("pipe", None, None),
        P("pipe", None),
        P("pipe", None, None),
        P("pipe", None),
        P("pipe", None),
        P(("pipe", "dp"), None),
        P("dp", None),
    )
    out_specs = (
        P("pipe", "dp", None, None),
        P(("pipe", "dp")),
        P("dp"),
        P(("pipe", "dp"), None),
        P("dp", None),
    )
    return jax.shard_map(local, mesh=mesh, in_specs=in_specs, out_specs=out_specs, check_vma=False)
```

time: 1280 us -> 67.6 us (0.05)
  waiting for transfers between devices: 1030 us -> 0 us
  matrix products: 134 us -> 0 us
  Pallas kernels: 0 us -> 61.7 us
  other arithmetic: 58.5 us -> 0 us
  between operations: 13.9 us -> 0.68 us
    reduce_scatter x1 -> x0, waiting for transfers between devices: 567 us -> none  [local(): lax.psum_scatter(100.0 * jnp.einsum('rt,re->te', dlogits, image_unit, pre...]
    all_gather x3 -> x0, waiting for transfers between devices: 420 us -> none  [the longest x1 216 us: local(): all_text = lax.all_gather(text_unit, 'dp', axis=0, tiled=True)]
    conv_general_dilated x3 -> x0, matrix products: 72.2 us -> none  [convnext_block(): lax.conv_general_dilated(grid, kernel, (1, 1), ((width // 2, width // 2),...]
    dot_general x6 -> x0, matrix products: 61.9 us -> none  [the longest x3 55.2 us: convnext_block(): jnp.dot(hidden, w_out, preferred_element_type=jnp.float32)]
    pallas_call x0 -> x1, Pallas kernels: none -> 61.7 us  [local(): pl.pallas_call(kernel, out_shape=(jax.ShapeDtypeStruct((1,) + images.shap...]
    reduce_sum x6 -> x0, other arithmetic: 49 us -> none  [the longest x3 46 us: convnext_block(): spread = jnp.mean(center * center, axis=1, keepdims=True)]
    ppermute x3 -> x0, waiting for transfers between devices: 42.3 us -> none  [passed_along(): return lax.ppermute(block, axis, route)]
  transfers between devices with their start and end apart: 7 -> 0, of which waited for: 7 -> 0; matrix products, arithmetic and copies ran while one was open for 0% -> 0% of each run, Pallas kernels for 0% -> 0%
where the time goes in v1:
time: 67.6 us; the launch traced here: 67.4 us
  Pallas kernels  61.7 us (91%)
  local copies, waits for them, and re-layouts  4.98 us (7%)
  between operations  0.68 us (1%)
    pallas_call x1, Pallas kernels, local(): pl.pallas_call(kernel, out_shape=(jax.ShapeDtypeStruct((1,) + images.shap...  61.7 us
    unnamed x13, local copies, waits for them, and re-layouts  4.98 us

profile of v1, /device:TPU:6, one launch (start us, length us, event | category | flops | bytes accessed | tf_op | source)
XLA Modules:
  0.0 67.4 jit_solution(6819588480601426828)
XLA Ops:
  0.6 61.7 %sections_and_loss.1 = (bf16[1,2,1024,384]{3,2,1,0:T(8,128)(2,1)}, f32[1,4]{1,0:T(1,128)}, f32[1,8]{1,0:T(1,128)}, f32[4,1024]{1,0:T(4,128)}, f32[8,1024]{1,0:T(8,128)}) custom-call(bf16[2,1024,384]{2,1,0:T(8,128)(2,1)} %images.1, bf16[1,49,384]{2,1,0:T(8,128)(2,1)} %dw_kernel.1, bf16[1,384]{1,0:T(2,128)(2,1)} %dw_bias.1, bf16[1,384]{1,0:T(2,128)(2,1)} %norm_gain.1, ...), custom_call_target="tpu_custom_call" | custom-call | tf_op jit(solution)/shard_map/sections_and_loss/pallas_call | solution.py:356
  62.4 0.0 copy-start.3
  62.4 0.0 copy-start.2
  62.4 0.0 copy-start.1
  62.4 0.0 copy-start
  62.4 2.7 %copy.22 = bf16[1,2,1024,384]{3,2,1,0:T(8,128)(2,1)} copy(bf16[1,2,1024,384]{3,2,1,0:T(8,128)(2,1)} %get-tuple-element.20) | data formatting | bytes 3145728
  65.1 0.0 copy-done.3
  65.1 0.5 copy.23
  65.7 0.0 copy-done.2
  65.7 0.5 copy.24
  66.2 0.0 copy-done.1
  66.2 0.6 copy.25
  66.8 0.0 copy-done
  66.8 0.6 copy.26
Async XLA Ops:
  62.4 2.8 %copy-start.3 = (f32[1,4]{1,0:T(1,128)S(1)}, f32[1,4]{1,0:T(1,128)}, u32[]{:S(2)}) copy-start(f32[1,4]{1,0:T(1,128)} %get-tuple-element.11) | copy-start | bytes 52
  62.4 3.3 %copy-start.2 = (f32[1,8]{1,0:T(1,128)S(1)}, f32[1,8]{1,0:T(1,128)}, u32[]{:S(2)}) copy-start(f32[1,8]{1,0:T(1,128)} %get-tuple-element.12) | copy-start | bytes 100
  62.4 3.8 %copy-start.1 = (f32[4,1024]{1,0:T(4,128)S(1)}, f32[4,1024]{1,0:T(4,128)}, u32[]{:S(2)}) copy-start(f32[4,1024]{1,0:T(4,128)} %get-tuple-element.23) | copy-start | bytes 49156
  62.4 4.4 %copy-start = (f32[8,1024]{1,0:T(8,128)S(1)}, f32[8,1024]{1,0:T(8,128)}, u32[]{:S(2)}) copy-start(f32[8,1024]{1,0:T(8,128)} %get-tuple-element.24) | copy-start | bytes 98308

commit v2 on v1

--- a/solution.py
+++ b/solution.py
@@ -15,7 +15,7 @@
 GROUP = 16
 SIDE = 32
 LANES = 128
-STRIP = 8
+STRIP = 4
 STRIPS = SIDE // STRIP
 POS = STRIP * SIDE
 LEFT = 8
@@ -295,20 +295,8 @@
     load_a.wait()
     load_b.wait()
 
-    def step(k, carry):
+    def strip(k):
         i, s = lax.div(k, STRIPS), lax.rem(k, STRIPS)
-
-        @pl.when(k == 2 - 2 * sec)
-        def _():
-            loss_logits()
-
-        @pl.when(k == 4 - 3 * sec)
-        def _():
-            loss_grads()
-
-        @pl.when(k == 6 - 3 * sec)
-        def _():
-            loss_sums()
 
         @pl.when(s == 0)
         def _():
@@ -323,9 +311,23 @@
         def _():
             strip_copy(k).start()
         store_copy(k).start()
+
+    def step(k, carry):
+        @pl.when(k == 1 - sec)
+        def _():
+            loss_logits()
+
+        @pl.when(k == total * (1 - sec))
+        def _():
+            loss_grads()
+            loss_sums()
+
+        @pl.when(k < total)
+        def _():
+            strip(k)
         return carry
 
-    lax.fori_loop(0, total, step, 0)
+    lax.fori_loop(0, total + 1, step, 0)
 
     half_copy.wait_send()
     half_copy.wait_recv()

time: 67.6 us -> 67.4 us (level); the launches traced: 67.4 us -> 66.5 us
  Pallas kernels: 61.7 us -> 60.8 us
    pallas_call x1, Pallas kernels: 61.7 us -> 60.8 us  [local(): pl.pallas_call(kernel, out_shape=(jax.ShapeDtypeStruct((1,) + images.shap...]
where the time goes in v2:
time: 67.4 us; the launch traced here: 66.5 us
  Pallas kernels  60.8 us (90%)
  local copies, waits for them, and re-layouts  4.98 us (7%)
  between operations  0.68 us (1%)
    pallas_call x1, Pallas kernels, local(): pl.pallas_call(kernel, out_shape=(jax.ShapeDtypeStruct((1,) + images.shap...  60.8 us
    unnamed x13, local copies, waits for them, and re-layouts  4.98 us

profile of v2, /device:TPU:6, one launch (start us, length us, event | category | flops | bytes accessed | tf_op | source)
XLA Modules:
  0.0 66.5 jit_solution(3552480701108216079)
XLA Ops:
  0.6 60.8 %sections_and_loss.1 = (bf16[1,2,1024,384]{3,2,1,0:T(8,128)(2,1)}, f32[1,4]{1,0:T(1,128)}, f32[1,8]{1,0:T(1,128)}, f32[4,1024]{1,0:T(4,128)}, f32[8,1024]{1,0:T(8,128)}) custom-call(bf16[2,1024,384]{2,1,0:T(8,128)(2,1)} %images.1, bf16[1,49,384]{2,1,0:T(8,128)(2,1)} %dw_kernel.1, bf16[1,384]{1,0:T(2,128)(2,1)} %dw_bias.1, bf16[1,384]{1,0:T(2,128)(2,1)} %norm_gain.1, ...), custom_call_target="tpu_custom_call" | custom-call | tf_op jit(solution)/shard_map/sections_and_loss/pallas_call | solution.py:358
  61.5 0.0 copy-start.3
  61.5 0.0 copy-start.2
  61.5 0.0 copy-start.1
  61.5 0.0 copy-start
  61.5 2.7 %copy.22 = bf16[1,2,1024,384]{3,2,1,0:T(8,128)(2,1)} copy(bf16[1,2,1024,384]{3,2,1,0:T(8,128)(2,1)} %get-tuple-element.20) | data formatting | bytes 3145728
  64.2 0.0 copy-done.3
  64.2 0.5 copy.23
  64.8 0.0 copy-done.2
  64.8 0.5 copy.24
  65.3 0.0 copy-done.1
  65.3 0.6 copy.25
  65.9 0.0 copy-done
  65.9 0.6 copy.26
Async XLA Ops:
  61.5 2.8 %copy-start.3 = (f32[1,4]{1,0:T(1,128)S(1)}, f32[1,4]{1,0:T(1,128)}, u32[]{:S(2)}) copy-start(f32[1,4]{1,0:T(1,128)} %get-tuple-element.11) | copy-start | bytes 52
  61.5 3.3 %copy-start.2 = (f32[1,8]{1,0:T(1,128)S(1)}, f32[1,8]{1,0:T(1,128)}, u32[]{:S(2)}) copy-start(f32[1,8]{1,0:T(1,128)} %get-tuple-element.12) | copy-start | bytes 100
  61.5 3.8 %copy-start.1 = (f32[4,1024]{1,0:T(4,128)S(1)}, f32[4,1024]{1,0:T(4,128)}, u32[]{:S(2)}) copy-start(f32[4,1024]{1,0:T(4,128)} %get-tuple-element.23) | copy-start | bytes 49156
  61.5 4.4 %copy-start = (f32[8,1024]{1,0:T(8,128)S(1)}, f32[8,1024]{1,0:T(8,128)}, u32[]{:S(2)}) copy-start(f32[8,1024]{1,0:T(8,128)} %get-tuple-element.24) | copy-start | bytes 98308

commit v3 on v2

--- a/solution.py
+++ b/solution.py
@@ -15,7 +15,7 @@
 GROUP = 16
 SIDE = 32
 LANES = 128
-STRIP = 4
+STRIP = 8
 STRIPS = SIDE // STRIP
 POS = STRIP * SIDE
 LEFT = 8

time: 67.4 us -> 67.4 us (level); the launches traced: 66.5 us -> 67.2 us
  Pallas kernels: 60.8 us -> 61.5 us
    pallas_call x1, Pallas kernels: 60.8 us -> 61.5 us  [local(): pl.pallas_call(kernel, out_shape=(jax.ShapeDtypeStruct((1,) + images.shap...]
where the time goes in v3:
time: 67.4 us; the launch traced here: 67.2 us
  Pallas kernels  61.5 us (91%)
  local copies, waits for them, and re-layouts  4.98 us (7%)
  between operations  0.68 us (1%)
    pallas_call x1, Pallas kernels, local(): pl.pallas_call(kernel, out_shape=(jax.ShapeDtypeStruct((1,) + images.shap...  61.5 us
    unnamed x13, local copies, waits for them, and re-layouts  4.98 us

profile of v3, /device:TPU:6, one launch (start us, length us, event | category | flops | bytes accessed | tf_op | source)
XLA Modules:
  0.0 67.2 jit_solution(1014296717233831285)
XLA Ops:
  0.6 61.5 %sections_and_loss.1 = (bf16[1,2,1024,384]{3,2,1,0:T(8,128)(2,1)}, f32[1,4]{1,0:T(1,128)}, f32[1,8]{1,0:T(1,128)}, f32[4,1024]{1,0:T(4,128)}, f32[8,1024]{1,0:T(8,128)}) custom-call(bf16[2,1024,384]{2,1,0:T(8,128)(2,1)} %images.1, bf16[1,49,384]{2,1,0:T(8,128)(2,1)} %dw_kernel.1, bf16[1,384]{1,0:T(2,128)(2,1)} %dw_bias.1, bf16[1,384]{1,0:T(2,128)(2,1)} %norm_gain.1, ...), custom_call_target="tpu_custom_call" | custom-call | tf_op jit(solution)/shard_map/sections_and_loss/pallas_call | solution.py:358
  62.2 0.0 copy-start.3
  62.2 0.0 copy-start.2
  62.2 0.0 copy-start.1
  62.2 0.0 copy-start
  62.2 2.7 %copy.22 = bf16[1,2,1024,384]{3,2,1,0:T(8,128)(2,1)} copy(bf16[1,2,1024,384]{3,2,1,0:T(8,128)(2,1)} %get-tuple-element.20) | data formatting | bytes 3145728
  64.9 0.0 copy-done.3
  64.9 0.5 copy.23
  65.5 0.0 copy-done.2
  65.5 0.5 copy.24
  66.0 0.0 copy-done.1
  66.0 0.6 copy.25
  66.6 0.0 copy-done
  66.6 0.6 copy.26
Async XLA Ops:
  62.2 2.8 %copy-start.3 = (f32[1,4]{1,0:T(1,128)S(1)}, f32[1,4]{1,0:T(1,128)}, u32[]{:S(2)}) copy-start(f32[1,4]{1,0:T(1,128)} %get-tuple-element.11) | copy-start | bytes 52
  62.2 3.3 %copy-start.2 = (f32[1,8]{1,0:T(1,128)S(1)}, f32[1,8]{1,0:T(1,128)}, u32[]{:S(2)}) copy-start(f32[1,8]{1,0:T(1,128)} %get-tuple-element.12) | copy-start | bytes 100
  62.2 3.8 %copy-start.1 = (f32[4,1024]{1,0:T(4,128)S(1)}, f32[4,1024]{1,0:T(4,128)}, u32[]{:S(2)}) copy-start(f32[4,1024]{1,0:T(4,128)} %get-tuple-element.23) | copy-start | bytes 49156
  62.2 4.4 %copy-start = (f32[8,1024]{1,0:T(8,128)S(1)}, f32[8,1024]{1,0:T(8,128)}, u32[]{:S(2)}) copy-start(f32[8,1024]{1,0:T(8,128)} %get-tuple-element.24) | copy-start | bytes 98308

commit v4 on v3

--- a/solution.py
+++ b/solution.py
@@ -241,29 +241,27 @@
                 v[:, c * LANES:(c + 1) * LANES].reshape(STRIP, SIDE, LANES))
 
     def block(i, s):
-        half = 4
-
-        def convolve(n, carry):
-            c, h = lax.div(n, STRIP // half), lax.rem(n, STRIP // half)
-            acc = jnp.zeros((half, 4, 8, LANES), F32)
-            for dw in range(7):
-                start = LEFT - 3 + dw
-                xs = xpad[i, c, pl.ds(STRIP * s + half * h, half + 6), start:start + SIDE]
-                xs = xs.reshape(half + 6, 4, 8, LANES)
-                for dh in range(7):
-                    acc = acc + xs[dh:dh + half] * taps[c, dh * 7 + dw]
-            rows = pl.ds(pl.multiple_of(h * half * SIDE, half * SIDE), half * SIDE)
-            conv[c, rows] = acc.reshape(half * SIDE, LANES)
+        def convolve(c, carry):
+            for w in range(0, SIDE, 16):
+                acc = jnp.zeros((STRIP, 2, 8, LANES), F32)
+                for dw in range(7):
+                    start = LEFT - 3 + dw + w
+                    xs = xpad[i, c, pl.ds(STRIP * s, STRIP + 6), start:start + 16]
+                    xs = xs.reshape(STRIP + 6, 2, 8, LANES)
+                    for dh in range(7):
+                        acc = acc + xs[dh:dh + STRIP] * taps[c, dh * 7 + dw]
+                conv[c, :, w:w + 16] = acc.reshape(STRIP, 16, LANES)
             return carry
 
-        lax.fori_loop(0, tiles * (STRIP // half), convolve, 0)
+        lax.fori_loop(0, tiles, convolve, 0)
 
         def part(ref, c):
             return ref[0:1, c * LANES:(c + 1) * LANES].astype(F32)
 
         for q in range(4):
             rows = slice(q * POS // 4, (q + 1) * POS // 4)
-            v = [conv[c, rows] + part(dw_bias, c) for c in range(tiles)]
+            v = [conv[c, q * STRIP // 4:(q + 1) * STRIP // 4].reshape(POS // 4, LANES) + part(dw_bias, c)
+                 for c in range(tiles)]
             mean = jnp.sum(functools.reduce(jnp.add, v), axis=1, keepdims=True) * (1.0 / channels)
             v = [a - mean for a in v]
             var = jnp.sum(functools.reduce(jnp.add, [a * a for a in v]), axis=1, keepdims=True) * (1.0 / channels)
@@ -371,7 +369,7 @@
             pltpu.VMEM(images.shape, BF16),
             pltpu.VMEM((micro, tiles, SIDE + 6, LEFT + SIDE + 8, LANES), F32),
             pltpu.VMEM((tiles, 49, 8, LANES), F32),
-            pltpu.VMEM((tiles, POS, LANES), F32),
+            pltpu.VMEM((tiles, STRIP, SIDE, LANES), F32),
             pltpu.VMEM((POS, channels), BF16),
             pltpu.VMEM((POS, channels), F32),
             pltpu.VMEM((channels, hidden), BF16),

time: 67.4 us -> 67.1 us (level)
  no operation moved by 1% of the time
where the time goes in v4:
time: 67.1 us; the launch traced here: 66.9 us
  Pallas kernels  61.2 us (91%)
  local copies, waits for them, and re-layouts  4.98 us (7%)
  between operations  0.68 us (1%)
    pallas_call x1, Pallas kernels, local(): pl.pallas_call(kernel, out_shape=(jax.ShapeDtypeStruct((1,) + images.shap...  61.2 us
    unnamed x13, local copies, waits for them, and re-layouts  4.98 us

profile of v4, /device:TPU:6, one launch (start us, length us, event | category | flops | bytes accessed | tf_op | source)
XLA Modules:
  0.0 66.9 jit_solution(2340567613852778074)
XLA Ops:
  0.6 61.2 %sections_and_loss.1 = (bf16[1,2,1024,384]{3,2,1,0:T(8,128)(2,1)}, f32[1,4]{1,0:T(1,128)}, f32[1,8]{1,0:T(1,128)}, f32[4,1024]{1,0:T(4,128)}, f32[8,1024]{1,0:T(8,128)}) custom-call(bf16[2,1024,384]{2,1,0:T(8,128)(2,1)} %images.1, bf16[1,49,384]{2,1,0:T(8,128)(2,1)} %dw_kernel.1, bf16[1,384]{1,0:T(2,128)(2,1)} %dw_bias.1, bf16[1,384]{1,0:T(2,128)(2,1)} %norm_gain.1, ...), custom_call_target="tpu_custom_call" | custom-call | tf_op jit(solution)/shard_map/sections_and_loss/pallas_call | solution.py:356
  61.9 0.0 copy-start.3
  61.9 0.0 copy-start.2
  61.9 0.0 copy-start.1
  61.9 0.0 copy-start
  61.9 2.7 %copy.22 = bf16[1,2,1024,384]{3,2,1,0:T(8,128)(2,1)} copy(bf16[1,2,1024,384]{3,2,1,0:T(8,128)(2,1)} %get-tuple-element.20) | data formatting | bytes 3145728
  64.6 0.0 copy-done.3
  64.7 0.5 copy.23
  65.2 0.0 copy-done.2
  65.2 0.5 copy.24
  65.7 0.0 copy-done.1
  65.7 0.6 copy.25
  66.3 0.0 copy-done
  66.3 0.6 copy.26
Async XLA Ops:
  61.9 2.8 %copy-start.3 = (f32[1,4]{1,0:T(1,128)S(1)}, f32[1,4]{1,0:T(1,128)}, u32[]{:S(2)}) copy-start(f32[1,4]{1,0:T(1,128)} %get-tuple-element.11) | copy-start | bytes 52
  61.9 3.3 %copy-start.2 = (f32[1,8]{1,0:T(1,128)S(1)}, f32[1,8]{1,0:T(1,128)}, u32[]{:S(2)}) copy-start(f32[1,8]{1,0:T(1,128)} %get-tuple-element.12) | copy-start | bytes 100
  61.9 3.8 %copy-start.1 = (f32[4,1024]{1,0:T(4,128)S(1)}, f32[4,1024]{1,0:T(4,128)}, u32[]{:S(2)}) copy-start(f32[4,1024]{1,0:T(4,128)} %get-tuple-element.23) | copy-start | bytes 49156
  61.9 4.4 %copy-start = (f32[8,1024]{1,0:T(8,128)S(1)}, f32[8,1024]{1,0:T(8,128)}, u32[]{:S(2)}) copy-start(f32[8,1024]{1,0:T(8,128)} %get-tuple-element.24) | copy-start | bytes 98308
